TPU v7x, 32 devices: a whole 2x2x4 slice. The times are simulated.
32 devices in a mesh: groups: 2 (over y), obs: 4 (over z), hid: 2 (over x), rep: 2 (over core).
Axes of the slice: x: 2, y: 2, z: 4, core: 2. Of those that a mesh axis runs over, the one named last changes fastest.
Arguments:
- particles: float32 [8, 128, 512], P(('groups', 'obs')), parts along dimension 0, may hold values from -6 to 6
- obs_embed: bfloat16 [32768, 256], P(('groups', 'obs', 'rep')), parts along dimension 0, may hold values from -6 to 6
- step_index: int32 [2], P('groups'), parts along dimension 0, may hold values from 1 to 63
- noise: float32 [8, 128, 512], P('groups', 'obs'), parts along dimension 0, may hold values from -6 to 6
- w_query: bfloat16 [512, 2048], P(None, 'hid'), may hold values from -0.25 to 0.25
- w_key: bfloat16 [256, 2048], P(None, 'hid'), may hold values from -0.375 to 0.375
- w_value: bfloat16 [256, 2048], P(None, 'hid'), may hold values from -0.375 to 0.375
- w_time: bfloat16 [256, 16], P(None, 'hid'), may hold values from -0.375 to 0.375
- w_score: bfloat16 [2048, 512], P('hid'), may hold values from -0.0009765625 to 0.0009765625
- prior_in: bfloat16 [512, 2048], P(None, 'hid'), may hold values from -0.25 to 0.25
- prior_time: bfloat16 [256, 2048], P(None, 'hid'), may hold values from -0.375 to 0.375
- prior_out: bfloat16 [2048, 512], P('hid'), may hold values from -7.6293945e-06 to 7.6293945e-06
Outputs:
- updated: float32 [8, 128, 512], P('groups', 'obs'), parts along dimension 0
- score_total: float32 [8, 128, 512], P('groups', 'obs'), parts along dimension 0
There are 2 independent parts, one for each index of `groups`. A program takes and returns all parts, laid end to end along the dimension named above; an argument that names none is the same for every part. Nothing has to cross between parts.
All inputs are finite; a program needn't handle non-finite values.
Results may differ from a plain program's by a relative error of at most 0.0042.
Values may be sent and summed in bfloat16 or wider, within the bound.
No kernel may reach another device: no remote copies, remote signals or barrier semaphores. Data moves between devices by JAX's collectives and lax.ppermute only.
A program may use at most 64 MiB of HBM per device.

v0:
```python
import math
import jax
import jax.numpy as jnp
from jax import lax
from jax.sharding import PartitionSpec as P

DH = 128
STEPS = 64
SIG_LO = 0.05
SIG_HI = 1.0


def passed_along(shard, axis, by):
    size = lax.axis_size(axis)
    return lax.ppermute(shard, axis, [(i, (i + by) % size) for i in range(size)])


def plan(step_index, feature_count):
    level = step_index[0].astype(jnp.float32)
    growth = math.log(SIG_HI / SIG_LO) / (STEPS - 1)
    sigma_now = SIG_LO * jnp.exp(growth * level)
    sigma_prev = SIG_LO * jnp.exp(growth * (level - 1.0))
    delta = sigma_now * sigma_now - sigma_prev * sigma_prev
    halves = feature_count // 2
    frequency = jnp.exp(-math.log(1000.0) / halves * jnp.arange(halves).astype(jnp.float32))
    angles = 10.0 * jnp.log(sigma_now) * frequency
    features = jnp.concatenate([jnp.sin(angles), jnp.cos(angles)])[None, :].astype(jnp.bfloat16)
    return (features, delta)


def pair_pool(queries, keys, values, head_bias):
    count = queries.shape[0]
    query_heads = queries.reshape(count, -1, DH)
    key_heads = keys.reshape(keys.shape[0], -1, DH)
    value_heads = values.reshape(values.shape[0], -1, DH)
    scores = jnp.einsum("phd,jhd->phj", query_heads, key_heads, preferred_element_type=jnp.float32)
    weights = jax.nn.silu(scores * (1.0 / math.sqrt(DH)) + head_bias[None, :, None]).astype(
        jnp.bfloat16
    )
    pooled = jnp.einsum("phj,jhd->phd", weights, value_heads, preferred_element_type=jnp.float32)
    return pooled.reshape(count, -1)


def on_device(
    particles,
    obs_embed,
    step_index,
    noise,
    w_query,
    w_key,
    w_value,
    w_time,
    w_score,
    prior_in,
    prior_time,
    prior_out,
):
    obs_count = lax.axis_size("obs")
    rep_count = lax.axis_size("rep")
    features, delta = plan(step_index, w_time.shape[0])
    head_bias = jnp.dot(features, w_time, preferred_element_type=jnp.float32)[0]
    keys = jnp.dot(obs_embed, w_key, preferred_element_type=jnp.float32).astype(jnp.bfloat16)
    values = jnp.dot(obs_embed, w_value, preferred_element_type=jnp.float32).astype(jnp.bfloat16)
    home = particles[0]
    block_rows = home.shape[0]
    width = home.shape[1]
    stripe = block_rows // obs_count
    owned = home.reshape(obs_count, stripe, width)
    theta_owner = lax.all_to_all(owned, "obs", split_axis=0, concat_axis=0, tiled=True)
    moving = home.astype(jnp.bfloat16)

    def pool(travel):
        queries = jnp.dot(travel, w_query, preferred_element_type=jnp.float32).astype(jnp.bfloat16)
        return pair_pool(queries, keys, values, head_bias)

    score_weight = w_score.astype(jnp.float32)

    def turn(turn_index, cycle_state):
        arrived = passed_along(cycle_state[0], "obs", 1)
        totals = passed_along(cycle_state[1], "obs", 1)
        return (arrived, totals + pool(arrived))

    cycle_state = lax.fori_loop(0, obs_count - 1, turn, (moving, pool(moving)))
    pieces = cycle_state[1].reshape(obs_count, stripe, -1)
    flat = pieces.reshape(-1, pieces.shape[-1])
    result = jnp.dot(
        flat, score_weight, precision=lax.Precision.HIGHEST, preferred_element_type=jnp.float32
    )
    pieces = result.reshape(pieces.shape[:-1] + (width,))
    received = lax.all_to_all(pieces, "obs", split_axis=0, concat_axis=0, tiled=True)
    summed = jnp.roll(received, 1, axis=0)
    owner_rows = theta_owner.reshape(block_rows, width)
    share = block_rows // rep_count
    start = lax.axis_index("rep") * share
    my_rows = lax.dynamic_slice_in_dim(owner_rows, start, share, 0).astype(jnp.bfloat16)
    prior_pre = jnp.dot(my_rows, prior_in, preferred_element_type=jnp.float32) + jnp.dot(
        features, prior_time, preferred_element_type=jnp.float32
    )
    prior_hidden = jax.nn.silu(prior_pre).astype(jnp.bfloat16)
    prior_part = jnp.dot(prior_hidden, prior_out, preferred_element_type=jnp.float32)
    total_count = obs_embed.shape[0] * obs_count * rep_count
    scores_flat = summed.reshape(block_rows, width)
    current = lax.dynamic_slice_in_dim(scores_flat, start, share, 0)
    scores_flat = lax.dynamic_update_slice_in_dim(
        scores_flat, current - (total_count - 1) * prior_part, start, 0
    )
    score_total = lax.psum(scores_flat, ("hid", "rep")).reshape(obs_count, stripe, width)
    updated = theta_owner + delta * score_total + jnp.sqrt(delta) * noise
    return (updated, score_total)


def solution(mesh):
    in_specs = (
        P(("groups", "obs"), None, None),
        P(("groups", "obs", "rep"), None),
        P("groups"),
        P("groups", "obs", None),
        P(None, "hid"),
        P(None, "hid"),
        P(None, "hid"),
        P(None, "hid"),
        P("hid", None),
        P(None, "hid"),
        P(None, "hid"),
        P("hid", None),
    )
    out_specs = (P("groups", "obs", None), P("groups", "obs", None))
    return jax.shard_map(
        on_device, mesh=mesh, in_specs=in_specs, out_specs=out_specs, check_vma=False
    )
```

profile of v0, /device:TPU:0, one launch (start us, length us, event | category | flops | bytes accessed | tf_op | source)
XLA Modules:
  0.0 154.7 jit_solution(1549332694135412617)
XLA Ops:
  8.1 0.3 copy-done
  8.4 4.3 %convolution_convert_fusion.2 = bf16[2048,1024]{0,1:T(8,128)(2,1)} fusion(bf16[2048,256]{1,0:T(8,128)(2,1)S(1)} %copy-done, bf16[256,1024]{1,0:T(8,128)(2,1)} %param.20), kind=kOutput, calls=%fused_computation.23 | convolution fusion | flops 1075838976 | bytes 5767168 | tf_op jit(solution)/shard_map/dot_general | solution.py:63
  12.8 3.3 %convolution_convert_fusion.1 = bf16[2048,1024]{0,1:T(8,128)(2,1)} fusion(bf16[2048,256]{1,0:T(8,128)(2,1)S(1)} %copy-done, bf16[256,1024]{1,0:T(8,128)(2,1)S(1)} %copy-done.4), kind=kOutput, calls=%fused_computation.22 | convolution fusion | flops 1075838976 | bytes 5767168 | tf_op jit(solution)/shard_map/dot_general | solution.py:62
  16.1 6.5 %copy.19 = bf16[2048,1024]{1,0:T(8,128)(2,1)} copy(bf16[2048,1024]{0,1:T(8,128)(2,1)} %convolution_convert_fusion.1) | data formatting | bytes 8388608 | tf_op jit(solution)/shard_map/while | solution.py:83
  22.7 0.3 fusion.21
  23.0 8.8 %fusion.20 = f32[8,128,128]{2,1,0:T(8,128)} fusion(bf16[2048,8,128]{0,2,1:T(8,128)(2,1)} %bitcast.116, bf16[2048,8,128]{0,2,1:T(8,128)(2,1)} %bitcast.115, f32[8]{0:T(128)S(1)} %bitcast.124, bf16[16,8,8,128]{3,2,1,0:T(8,128)(2,1)S(1)} %fusion.21), kind=kOutput, calls=%fused_computation.24 | convolution fusion | flops 1088421888 | bytes 9175072 | tf_op jit(solution)/shard_map/phj,jhd->phd/dot_general | solution.py:40
  31.9 56.9 %while.12 = (s32[]{:T(128)}, bf16[128,512]{1,0:T(8,128)(2,1)S(1)}, f32[128,1024]{0,1:T(8,128)}, bf16[512,1024]{1,0:T(8,128)(2,1)S(1)}, bf16[2048,1024]{1,0:T(8,1...) while((s32[]{:T(128)}, bf16[128,512]{1,0:T(8,128)(2,1)S(1)}, ...), condition=%wide.region_1.2_spmd, body=%wide.region_0.1_spmd.sunk | while | flops 1222901760 | bytes 15073477 | solution.py:83
  31.9 3.0 %collective-permute-start = (bf16[128,512]{1,0:T(8,128)(2,1)S(1)}, bf16[128,512]{1,0:T(8,128)(2,1)S(1)}, u32[]{:S(2)}, u32[]{:S(2)}) collective-permute-start(bf16[128,512]{1,0:T(8,128)(2,1)S(1)} %get-tuple-element.115), channel_id=1, source_target_pairs={{0,4},{4,8},{8,12},{12,0},{1,5},{5,9},{9,13},{13,1},{2,6},{6,10},{... | collective-permute-start | bytes 393224 | tf_op jit(solution)/shard_map/while/body/eval_jaxpr/ppermute | solution.py:15
  34.9 1.6 %collective-permute-start.1 = (f32[128,1024]{0,1:T(8,128)}, f32[128,1024]{0,1:T(8,128)S(1)}, u32[]{:S(2)}, u32[]{:S(2)}) collective-permute-start(f32[128,1024]{0,1:T(8,128)} %get-tuple-element.116), channel_id=1, source_target_pairs={{0,4},{4,8},{8,12},{12,0},{1,5},{5,9},{9,13},{13,1},{2,6},{6,10},{... | collective-permute-start | bytes 1572872 | tf_op jit(solution)/shard_map/while/body/eval_jaxpr/ppermute | solution.py:15
  36.5 4.8 %collective-permute-done = bf16[128,512]{1,0:T(8,128)(2,1)S(1)} collective-permute-done((bf16[128,512]{1,0:T(8,128)(2,1)S(1)}, bf16[128,512]{1,0:T(8,128)(2,1)S(1)}, u32[]{:S(2)}, u32[]{:S(2)}) %collective-permute-start) | collective-permute-done | bytes 131104 | tf_op jit(solution)/shard_map/while/body/eval_jaxpr/ppermute | solution.py:15
  41.6 6.3 %fusion.73 = f32[8,128,128]{1,2,0:T(8,128)S(1)} fusion(bf16[2048,8,128]{0,2,1:T(8,128)(2,1)} %bitcast.117, f32[8]{0:T(128)S(1)} %bitcast.125, bf16[16,8,8,128]{3,2,1,0:T(8,128)(2,1)S(1)} %fusion.72, bf16[2048,1024]{1,0:T(8,128)(2,1)} %get-tuple-element.126), kind=kOutput, calls=%fused_computation.8.clone.1 | convolution fusion | flops 1088421888 | bytes 9175072 | tf_op jit(solution)/shard_map/while/body/eval_jaxpr/phj,jhd->phd/dot_general | solution.py:40
  47.9 3.8 %collective-permute-done.1 = f32[128,1024]{0,1:T(8,128)S(1)} collective-permute-done((f32[128,1024]{0,1:T(8,128)}, f32[128,1024]{0,1:T(8,128)S(1)}, u32[]{:S(2)}, u32[]{:S(2)}) %collective-permute-start.1) | collective-permute-done | bytes 524320 | tf_op jit(solution)/shard_map/while/body/eval_jaxpr/ppermute | solution.py:15
  51.6 0.9 bitcast_add_fusion.2
  52.5 1.3 collective-permute-start.1
  53.8 6.9 %collective-permute-done = bf16[128,512]{1,0:T(8,128)(2,1)S(1)} collective-permute-done((bf16[128,512]{1,0:T(8,128)(2,1)S(1)}, bf16[128,512]{1,0:T(8,128)(2,1)S(1)}, u32[]{:S(2)}, u32[]{:S(2)}) %collective-permute-start) | collective-permute-done | bytes 131104 | tf_op jit(solution)/shard_map/while/body/eval_jaxpr/ppermute | solution.py:15
  61.1 6.3 %fusion.73 = f32[8,128,128]{1,2,0:T(8,128)S(1)} fusion(bf16[2048,8,128]{0,2,1:T(8,128)(2,1)} %bitcast.117, f32[8]{0:T(128)S(1)} %bitcast.125, bf16[16,8,8,128]{3,2,1,0:T(8,128)(2,1)S(1)} %fusion.72, bf16[2048,1024]{1,0:T(8,128)(2,1)} %get-tuple-element.126), kind=kOutput, calls=%fused_computation.8.clone.1 | convolution fusion | flops 1088421888 | bytes 9175072 | tf_op jit(solution)/shard_map/while/body/eval_jaxpr/phj,jhd->phd/dot_general | solution.py:40
  67.4 2.9 %collective-permute-done.1 = f32[128,1024]{0,1:T(8,128)S(1)} collective-permute-done((f32[128,1024]{0,1:T(8,128)}, f32[128,1024]{0,1:T(8,128)S(1)}, u32[]{:S(2)}, u32[]{:S(2)}) %collective-permute-start.1) | collective-permute-done | bytes 524320 | tf_op jit(solution)/shard_map/while/body/eval_jaxpr/ppermute | solution.py:15
  70.2 0.9 bitcast_add_fusion.2
  71.1 8.2 %collective-permute-done = bf16[128,512]{1,0:T(8,128)(2,1)S(1)} collective-permute-done((bf16[128,512]{1,0:T(8,128)(2,1)S(1)}, bf16[128,512]{1,0:T(8,128)(2,1)S(1)}, u32[]{:S(2)}, u32[]{:S(2)}) %collective-permute-start) | collective-permute-done | bytes 131104 | tf_op jit(solution)/shard_map/while/body/eval_jaxpr/ppermute | solution.py:15
  79.7 6.3 %fusion.73 = f32[8,128,128]{1,2,0:T(8,128)S(1)} fusion(bf16[2048,8,128]{0,2,1:T(8,128)(2,1)} %bitcast.117, f32[8]{0:T(128)S(1)} %bitcast.125, bf16[16,8,8,128]{3,2,1,0:T(8,128)(2,1)S(1)} %fusion.72, bf16[2048,1024]{1,0:T(8,128)(2,1)} %get-tuple-element.126), kind=kOutput, calls=%fused_computation.8.clone.1 | convolution fusion | flops 1088421888 | bytes 9175072 | tf_op jit(solution)/shard_map/while/body/eval_jaxpr/phj,jhd->phd/dot_general | solution.py:40
  86.0 2.0 %collective-permute-done.1 = f32[128,1024]{0,1:T(8,128)S(1)} collective-permute-done((f32[128,1024]{0,1:T(8,128)}, f32[128,1024]{0,1:T(8,128)S(1)}, u32[]{:S(2)}, u32[]{:S(2)}) %collective-permute-start.1) | collective-permute-done | bytes 524320 | tf_op jit(solution)/shard_map/while/body/eval_jaxpr/ppermute | solution.py:15
  87.9 0.9 bitcast_add_fusion.2
  88.8 2.2 %fusion.36 = f32[128,512]{1,0:T(8,128)S(1)} fusion(f32[128,1024]{0,1:T(8,128)} %get-tuple-element.39, bf16[1024,512]{1,0:T(8,128)(2,1)} %param.22), kind=kOutput, calls=%fused_computation.49 | convolution fusion | flops 805306368 | bytes 1835008 | tf_op jit(solution)/shard_map/dot_general | solution.py:86
  91.0 9.5 %all_to_all.10 = f32[4,32,512]{2,1,0:T(8,128)S(1)} all-to-all(f32[4,32,512]{2,1,0:T(8,128)S(1)} %bitcast.119), channel_id=1, replica_groups=mesh['groups'=2,'obs'=4,'hid'=2,'rep'=2] {'obs'}, dimensions={0} | all-to-all | bytes 524288 | tf_op jit(solution)/shard_map/all_to_all | solution.py:90
  100.5 3.4 %all-to-all-start = ((f32[4,32,512]{2,1,0:T(8,128)}), f32[4,32,512]{2,1,0:T(8,128)S(1)}, u32[]{:S(2)}, u32[]{:S(2)}) async-start(f32[4,32,512]{2,1,0:T(8,128)} %bitcast.120), calls=%async_computation | async-start | bytes 524288 | tf_op jit(solution)/shard_map/all_to_all | solution.py:69
  103.9 1.2 fusion.37
  105.2 5.4 %all-to-all-done = f32[4,32,512]{2,1,0:T(8,128)S(1)} async-done(((f32[4,32,512]{2,1,0:T(8,128)}), f32[4,32,512]{2,1,0:T(8,128)S(1)}, u32[]{:S(2)}, u32[]{:S(2)}) %all-to-all-start) | async-done | bytes 262176 | tf_op jit(solution)/shard_map/all_to_all | solution.py:69
  110.6 1.7 %fusion.23 = f32[128,512]{1,0:T(8,128)S(1)} fusion(f32[128,512]{1,0:T(8,128)S(1)} %bitcast.121, s32[]{:T(128)S(6)} %select_n.2, bf16[1024,512]{1,0:T(8,128)(2,1)S(1)} %copy-done.6, bf16[512,1024]{1,0:T(8,128)(2,1)} %param.23, f32[1024]{0:T(1024)S(1)} %bitcast.123, f32[128,512]{1,0:T(8,128)S(1)} %bitcast.118), kind=kOutput, calls=%fused_computation.30 | convolution fusion | flops 134676480 | bytes 2429952 | tf_op jit(solution)/shard_map/dot_general | solution.py:100
  112.4 0.7 copy-done.3
  113.2 31.3 %all-reduce.2.cloned.1.call-done = f32[4,32,512]{2,1,0:T(8,128)} async-done(((f32[4,32,512]{2,1,0:T(8,128)}), f32[4,32,512]{2,1,0:T(8,128)}) %all-reduce.2.cloned.1.call-update) | async-done | bytes 262160 | tf_op jit(solution)/shard_map/psum | solution.py:107
  144.5 1.7 %multiply_add_fusion = f32[4,32,512]{2,1,0:T(8,128)} fusion(f32[4,32,512]{2,1,0:T(8,128)S(1)} %copy-done.5, f32[4,32,512]{2,1,0:T(8,128)S(1)} %all-to-all-done, f32[4,32,512]{2,1,0:T(8,128)} %all-reduce.2.cloned.1.call-done, f32[]{:T(128)S(6)} %sqrt.3, f32[]{:T(128)} %bitcast.6), kind=kLoop, calls=%fused_computation.34 | loop fusion | flops 262144 | bytes 1048584 | tf_op jit(solution)/shard_map/add | solution.py:108
  146.2 1.7 %copy.57 = f32[4,32,512]{2,1,0:T(8,128)} copy(f32[4,32,512]{2,1,0:T(8,128)} %all-reduce.2.cloned.1.call-done) | data formatting | bytes 524288
  (33 shorter events, 1.3 us)
Async XLA Ops:
  7.2 1.2 copy-start
  8.4 4.4 %copy-start.4 = (bf16[256,1024]{1,0:T(8,128)(2,1)S(1)}, bf16[256,1024]{1,0:T(8,128)(2,1)}, u32[]{:S(2)}) copy-start(bf16[256,1024]{1,0:T(8,128)(2,1)} %param.19) | copy-start | bytes 1572868
  12.8 3.3 %copy-start.2 = (f32[1,128,512]{2,1,0:T(8,128)S(1)}, f32[1,128,512]{2,1,0:T(8,128)}, u32[]{:S(2)}) copy-start(f32[1,128,512]{2,1,0:T(8,128)} %param.14) | copy-start | bytes 786436
  16.1 6.5 %copy-start.7 = (bf16[256,8]{0,1:T(8,128)(2,1)S(1)}, bf16[256,8]{0,1:T(8,128)(2,1)}, u32[]{:S(2)}) copy-start(bf16[256,8]{0,1:T(8,128)(2,1)} %param.21) | copy-start | bytes 12292
  16.1 6.6 %copy-start.1 = (bf16[512,1024]{1,0:T(8,128)(2,1)S(1)}, bf16[512,1024]{1,0:T(8,128)(2,1)}, u32[]{:S(2)}) copy-start(bf16[512,1024]{1,0:T(8,128)(2,1)} %param.18) | copy-start | bytes 3145732
  31.9 9.4 %collective-permute-start = (bf16[128,512]{1,0:T(8,128)(2,1)S(1)}, bf16[128,512]{1,0:T(8,128)(2,1)S(1)}, u32[]{:S(2)}, u32[]{:S(2)}) collective-permute-start(bf16[128,512]{1,0:T(8,128)(2,1)S(1)} %get-tuple-element.115), channel_id=1, source_target_pairs={{0,4},{4,8},{8,12},{12,0},{1,5},{5,9},{9,13},{13,1},{2,6},{6,10},{... | collective-permute-start | bytes 393224 | tf_op jit(solution)/shard_map/while/body/eval_jaxpr/ppermute | solution.py:15
  34.9 16.7 %collective-permute-start.1 = (f32[128,1024]{0,1:T(8,128)}, f32[128,1024]{0,1:T(8,128)S(1)}, u32[]{:S(2)}, u32[]{:S(2)}) collective-permute-start(f32[128,1024]{0,1:T(8,128)} %get-tuple-element.116), channel_id=1, source_target_pairs={{0,4},{4,8},{8,12},{12,0},{1,5},{5,9},{9,13},{13,1},{2,6},{6,10},{... | collective-permute-start | bytes 1572872 | tf_op jit(solution)/shard_map/while/body/eval_jaxpr/ppermute | solution.py:15
  52.5 8.2 %collective-permute-start = (bf16[128,512]{1,0:T(8,128)(2,1)S(1)}, bf16[128,512]{1,0:T(8,128)(2,1)S(1)}, u32[]{:S(2)}, u32[]{:S(2)}) collective-permute-start(bf16[128,512]{1,0:T(8,128)(2,1)S(1)} %get-tuple-element.115), channel_id=1, source_target_pairs={{0,4},{4,8},{8,12},{12,0},{1,5},{5,9},{9,13},{13,1},{2,6},{6,10},{... | collective-permute-start | bytes 393224 | tf_op jit(solution)/shard_map/while/body/eval_jaxpr/ppermute | solution.py:15
  52.5 17.7 %collective-permute-start.1 = (f32[128,1024]{0,1:T(8,128)}, f32[128,1024]{0,1:T(8,128)S(1)}, u32[]{:S(2)}, u32[]{:S(2)}) collective-permute-start(f32[128,1024]{0,1:T(8,128)} %get-tuple-element.116), channel_id=1, source_target_pairs={{0,4},{4,8},{8,12},{12,0},{1,5},{5,9},{9,13},{13,1},{2,6},{6,10},{... | collective-permute-start | bytes 1572872 | tf_op jit(solution)/shard_map/while/body/eval_jaxpr/ppermute | solution.py:15
  71.1 8.2 %collective-permute-start = (bf16[128,512]{1,0:T(8,128)(2,1)S(1)}, bf16[128,512]{1,0:T(8,128)(2,1)S(1)}, u32[]{:S(2)}, u32[]{:S(2)}) collective-permute-start(bf16[128,512]{1,0:T(8,128)(2,1)S(1)} %get-tuple-element.115), channel_id=1, source_target_pairs={{0,4},{4,8},{8,12},{12,0},{1,5},{5,9},{9,13},{13,1},{2,6},{6,10},{... | collective-permute-start | bytes 393224 | tf_op jit(solution)/shard_map/while/body/eval_jaxpr/ppermute | solution.py:15
  71.1 16.8 %collective-permute-start.1 = (f32[128,1024]{0,1:T(8,128)}, f32[128,1024]{0,1:T(8,128)S(1)}, u32[]{:S(2)}, u32[]{:S(2)}) collective-permute-start(f32[128,1024]{0,1:T(8,128)} %get-tuple-element.116), channel_id=1, source_target_pairs={{0,4},{4,8},{8,12},{12,0},{1,5},{5,9},{9,13},{13,1},{2,6},{6,10},{... | collective-permute-start | bytes 1572872 | tf_op jit(solution)/shard_map/while/body/eval_jaxpr/ppermute | solution.py:15
  88.8 21.9 %copy-start.6 = (bf16[1024,512]{1,0:T(8,128)(2,1)S(1)}, bf16[1024,512]{1,0:T(8,128)(2,1)}, u32[]{:S(2)}) copy-start(bf16[1024,512]{1,0:T(8,128)(2,1)} %param.25) | copy-start | bytes 3145732
  88.8 55.7 %copy-start.5 = (f32[4,32,512]{2,1,0:T(8,128)S(1)}, f32[4,32,512]{2,1,0:T(8,128)}, u32[]{:S(2)}) copy-start(f32[4,32,512]{2,1,0:T(8,128)} %param.17) | copy-start | bytes 786436
  100.5 10.2 %all-to-all-start = ((f32[4,32,512]{2,1,0:T(8,128)}), f32[4,32,512]{2,1,0:T(8,128)S(1)}, u32[]{:S(2)}, u32[]{:S(2)}) async-start(f32[4,32,512]{2,1,0:T(8,128)} %bitcast.120), calls=%async_computation | async-start | bytes 524288 | tf_op jit(solution)/shard_map/all_to_all | solution.py:69
  103.9 40.6 %all-reduce.2.cloned.1.call-start = ((), (), s32[]{:S(2)}) async-start(), calls=%async_computation.2 | async-start | bytes 524288 | tf_op jit(solution)/shard_map/psum | solution.py:107
  112.4 0.7 copy-start.3
Sparse Core Ops, SparseCore 0:
  113.2 31.2 all-reduce.1
where the time goes:
time: 155 us
  waiting for transfers between devices  65.3 us (42%)
  matrix products  41.7 us (27%)
  between operations  15.1 us (10%)
  blocking collectives  9.51 us (6%)
  starting transfers between devices  9.34 us (6%)
  local copies, waits for them, and re-layouts  9.31 us (6%)
  other arithmetic  4.42 us (3%)
    psum x1, waiting for transfers between devices, on_device(): lax.psum(scores_flat, ('hid', 'rep')).reshape(obs_count, stripe, width)  31.3 us
    ppermute x6, waiting for transfers between devices, passed_along(): lax.ppermute(shard, axis, [(i, (i + by) % size) for i in range(size)])  28.5 us
    dot_general x4, matrix products, pair_pool(): jnp.einsum('phj,jhd->phd', weights, value_heads, preferred_element_type=j...  27.6 us
    all_to_all x1, blocking collectives, on_device(): lax.all_to_all(pieces, 'obs', split_axis=0, concat_axis=0, tiled=True)  9.51 us
    while x1, local copies, waits for them, and re-layouts, on_device(): cycle_state = lax.fori_loop(0, obs_count - 1, turn, (moving, pool(moving)))  6.51 us
    ppermute x6, starting transfers between devices, passed_along(): lax.ppermute(shard, axis, [(i, (i + by) % size) for i in range(size)])  5.89 us
    all_to_all x1, waiting for transfers between devices, on_device(): lax.all_to_all(owned, 'obs', split_axis=0, concat_axis=0, tiled=True)  5.4 us
    dot_general x1, matrix products, on_device(): jnp.dot(obs_embed, w_value, preferred_element_type=jnp.float32)  4.35 us
  transfers between devices with their start and end apart: 8, of which 8 were waited for; matrix products, arithmetic and copies ran while one was open for 14% of the time, Pallas kernels for 0%

commit v1 on v0

--- a/solution.py
+++ b/solution.py
@@ -8,6 +8,11 @@
 STEPS = 64
 SIG_LO = 0.05
 SIG_HI = 1.0
+
+
+def gather_and_add(x, axis):
+    shards = lax.all_gather(x, axis)
+    return jnp.sum(shards, axis=0)
 
 
 def passed_along(shard, axis, by):
@@ -104,7 +109,7 @@
     scores_flat = lax.dynamic_update_slice_in_dim(
         scores_flat, current - (total_count - 1) * prior_part, start, 0
     )
-    score_total = lax.psum(scores_flat, ("hid", "rep")).reshape(obs_count, stripe, width)
+    score_total = gather_and_add(scores_flat, ("hid", "rep")).reshape(obs_count, stripe, width)
     updated = theta_owner + delta * score_total + jnp.sqrt(delta) * noise
     return (updated, score_total)
 

time: 155 us -> 139 us (0.90)
  waiting for transfers between devices: 65.3 us -> 50 us
  local copies, waits for them, and re-layouts: 9.31 us -> 7.66 us
    psum x1 -> x0, waiting for transfers between devices: 31.3 us -> none  [on_device(): lax.psum(scores_flat, ('hid', 'rep')).reshape(obs_count, stripe, width)]
    all_gather x0 -> x1, waiting for transfers between devices: none -> 16.1 us  [gather_and_add(): shards = lax.all_gather(x, axis)]
    unnamed x17 -> x19, local copies, waits for them, and re-layouts: 2.74 us -> 1.09 us
  transfers between devices with their start and end apart: 8 -> 8, of which waited for: 8 -> 8; matrix products, arithmetic and copies ran while one was open for 14% -> 15% of each run, Pallas kernels for 0% -> 0%
where the time goes in v1:
time: 139 us; the launch traced here: 138 us
  waiting for transfers between devices  50 us (36%)
  matrix products  41.8 us (30%)
  between operations  15.1 us (11%)
  blocking collectives  9.65 us (7%)
  starting transfers between devices  9.34 us (7%)
  local copies, waits for them, and re-layouts  7.66 us (6%)
  other arithmetic  4.84 us (3%)
    ppermute x6, waiting for transfers between devices, passed_along(): lax.ppermute(shard, axis, [(i, (i + by) % size) for i in range(size)])  28.5 us
    dot_general x4, matrix products, pair_pool(): jnp.einsum('phj,jhd->phd', weights, value_heads, preferred_element_type=j...  27.7 us
    all_gather x1, waiting for transfers between devices, gather_and_add(): shards = lax.all_gather(x, axis)  16.1 us
    all_to_all x1, blocking collectives, on_device(): lax.all_to_all(pieces, 'obs', split_axis=0, concat_axis=0, tiled=True)  9.65 us
    while x1, local copies, waits for them, and re-layouts, on_device(): cycle_state = lax.fori_loop(0, obs_count - 1, turn, (moving, pool(moving)))  6.51 us
    ppermute x6, starting transfers between devices, passed_along(): lax.ppermute(shard, axis, [(i, (i + by) % size) for i in range(size)])  5.89 us
    all_to_all x1, waiting for transfers between devices, on_device(): lax.all_to_all(owned, 'obs', split_axis=0, concat_axis=0, tiled=True)  5.37 us
    dot_general x1, matrix products, on_device(): jnp.dot(obs_embed, w_value, preferred_element_type=jnp.float32)  4.36 us
  transfers between devices with their start and end apart: 8, of which 8 were waited for; matrix products, arithmetic and copies ran while one was open for 15% of the time, Pallas kernels for 0%

profile of v1, /device:TPU:0, one launch (start us, length us, event | category | flops | bytes accessed | tf_op | source)
XLA Modules:
  0.0 138.4 jit_solution(13304637071774757218)
XLA Ops:
  8.1 0.3 copy-done
  8.4 4.4 %convolution_convert_fusion.2 = bf16[2048,1024]{0,1:T(8,128)(2,1)} fusion(bf16[2048,256]{1,0:T(8,128)(2,1)S(1)} %copy-done, bf16[256,1024]{1,0:T(8,128)(2,1)} %param.20), kind=kOutput, calls=%fused_computation.23 | convolution fusion | flops 1075838976 | bytes 5767168 | tf_op jit(solution)/shard_map/dot_general | solution.py:68
  12.8 3.3 %convolution_convert_fusion.1 = bf16[2048,1024]{0,1:T(8,128)(2,1)} fusion(bf16[2048,256]{1,0:T(8,128)(2,1)S(1)} %copy-done, bf16[256,1024]{1,0:T(8,128)(2,1)S(1)} %copy-done.5), kind=kOutput, calls=%fused_computation.22 | convolution fusion | flops 1075838976 | bytes 5767168 | tf_op jit(solution)/shard_map/dot_general | solution.py:67
  16.1 6.5 %copy.25 = bf16[2048,1024]{1,0:T(8,128)(2,1)} copy(bf16[2048,1024]{0,1:T(8,128)(2,1)} %convolution_convert_fusion.1) | data formatting | bytes 8388608 | tf_op jit(solution)/shard_map/while | solution.py:88
  22.7 0.3 fusion.21
  23.0 8.9 %fusion.20 = f32[8,128,128]{2,1,0:T(8,128)} fusion(bf16[2048,8,128]{0,2,1:T(8,128)(2,1)} %bitcast.121, bf16[2048,8,128]{0,2,1:T(8,128)(2,1)} %bitcast.120, f32[8]{0:T(128)S(1)} %bitcast.131, bf16[16,8,8,128]{3,2,1,0:T(8,128)(2,1)S(1)} %fusion.21), kind=kOutput, calls=%fused_computation.24 | convolution fusion | flops 1088421888 | bytes 9175072 | tf_op jit(solution)/shard_map/phj,jhd->phd/dot_general | solution.py:45
  31.9 56.9 %while.12 = (s32[]{:T(128)}, bf16[128,512]{1,0:T(8,128)(2,1)S(1)}, f32[128,1024]{0,1:T(8,128)}, bf16[512,1024]{1,0:T(8,128)(2,1)S(1)}, bf16[2048,1024]{1,0:T(8,1...) while((s32[]{:T(128)}, bf16[128,512]{1,0:T(8,128)(2,1)S(1)}, ...), condition=%wide.region_1.2_spmd, body=%wide.region_0.1_spmd.sunk | while | flops 1222901760 | bytes 15073477 | solution.py:88
  31.9 3.0 %collective-permute-start = (bf16[128,512]{1,0:T(8,128)(2,1)S(1)}, bf16[128,512]{1,0:T(8,128)(2,1)S(1)}, u32[]{:S(2)}, u32[]{:S(2)}) collective-permute-start(bf16[128,512]{1,0:T(8,128)(2,1)S(1)} %get-tuple-element.122), channel_id=1, source_target_pairs={{0,4},{4,8},{8,12},{12,0},{1,5},{5,9},{9,13},{13,1},{2,6},{6,10},{... | collective-permute-start | bytes 393224 | tf_op jit(solution)/shard_map/while/body/eval_jaxpr/ppermute | solution.py:20
  34.9 1.6 %collective-permute-start.1 = (f32[128,1024]{0,1:T(8,128)}, f32[128,1024]{0,1:T(8,128)S(1)}, u32[]{:S(2)}, u32[]{:S(2)}) collective-permute-start(f32[128,1024]{0,1:T(8,128)} %get-tuple-element.123), channel_id=1, source_target_pairs={{0,4},{4,8},{8,12},{12,0},{1,5},{5,9},{9,13},{13,1},{2,6},{6,10},{... | collective-permute-start | bytes 1572872 | tf_op jit(solution)/shard_map/while/body/eval_jaxpr/ppermute | solution.py:20
  36.5 4.8 %collective-permute-done = bf16[128,512]{1,0:T(8,128)(2,1)S(1)} collective-permute-done((bf16[128,512]{1,0:T(8,128)(2,1)S(1)}, bf16[128,512]{1,0:T(8,128)(2,1)S(1)}, u32[]{:S(2)}, u32[]{:S(2)}) %collective-permute-start) | collective-permute-done | bytes 131104 | tf_op jit(solution)/shard_map/while/body/eval_jaxpr/ppermute | solution.py:20
  41.6 6.3 %fusion.74 = f32[8,128,128]{1,2,0:T(8,128)S(1)} fusion(bf16[2048,8,128]{0,2,1:T(8,128)(2,1)} %bitcast.122, f32[8]{0:T(128)S(1)} %bitcast.132, bf16[16,8,8,128]{3,2,1,0:T(8,128)(2,1)S(1)} %fusion.73, bf16[2048,1024]{1,0:T(8,128)(2,1)} %get-tuple-element.133), kind=kOutput, calls=%fused_computation.8.clone.1 | convolution fusion | flops 1088421888 | bytes 9175072 | tf_op jit(solution)/shard_map/while/body/eval_jaxpr/phj,jhd->phd/dot_general | solution.py:45
  47.9 3.8 %collective-permute-done.1 = f32[128,1024]{0,1:T(8,128)S(1)} collective-permute-done((f32[128,1024]{0,1:T(8,128)}, f32[128,1024]{0,1:T(8,128)S(1)}, u32[]{:S(2)}, u32[]{:S(2)}) %collective-permute-start.1) | collective-permute-done | bytes 524320 | tf_op jit(solution)/shard_map/while/body/eval_jaxpr/ppermute | solution.py:20
  51.7 0.9 bitcast_add_fusion.2
  52.6 1.3 collective-permute-start.1
  53.8 6.9 %collective-permute-done = bf16[128,512]{1,0:T(8,128)(2,1)S(1)} collective-permute-done((bf16[128,512]{1,0:T(8,128)(2,1)S(1)}, bf16[128,512]{1,0:T(8,128)(2,1)S(1)}, u32[]{:S(2)}, u32[]{:S(2)}) %collective-permute-start) | collective-permute-done | bytes 131104 | tf_op jit(solution)/shard_map/while/body/eval_jaxpr/ppermute | solution.py:20
  61.1 6.3 %fusion.74 = f32[8,128,128]{1,2,0:T(8,128)S(1)} fusion(bf16[2048,8,128]{0,2,1:T(8,128)(2,1)} %bitcast.122, f32[8]{0:T(128)S(1)} %bitcast.132, bf16[16,8,8,128]{3,2,1,0:T(8,128)(2,1)S(1)} %fusion.73, bf16[2048,1024]{1,0:T(8,128)(2,1)} %get-tuple-element.133), kind=kOutput, calls=%fused_computation.8.clone.1 | convolution fusion | flops 1088421888 | bytes 9175072 | tf_op jit(solution)/shard_map/while/body/eval_jaxpr/phj,jhd->phd/dot_general | solution.py:45
  67.4 2.9 %collective-permute-done.1 = f32[128,1024]{0,1:T(8,128)S(1)} collective-permute-done((f32[128,1024]{0,1:T(8,128)}, f32[128,1024]{0,1:T(8,128)S(1)}, u32[]{:S(2)}, u32[]{:S(2)}) %collective-permute-start.1) | collective-permute-done | bytes 524320 | tf_op jit(solution)/shard_map/while/body/eval_jaxpr/ppermute | solution.py:20
  70.3 0.9 bitcast_add_fusion.2
  71.2 8.2 %collective-permute-done = bf16[128,512]{1,0:T(8,128)(2,1)S(1)} collective-permute-done((bf16[128,512]{1,0:T(8,128)(2,1)S(1)}, bf16[128,512]{1,0:T(8,128)(2,1)S(1)}, u32[]{:S(2)}, u32[]{:S(2)}) %collective-permute-start) | collective-permute-done | bytes 131104 | tf_op jit(solution)/shard_map/while/body/eval_jaxpr/ppermute | solution.py:20
  79.7 6.3 %fusion.74 = f32[8,128,128]{1,2,0:T(8,128)S(1)} fusion(bf16[2048,8,128]{0,2,1:T(8,128)(2,1)} %bitcast.122, f32[8]{0:T(128)S(1)} %bitcast.132, bf16[16,8,8,128]{3,2,1,0:T(8,128)(2,1)S(1)} %fusion.73, bf16[2048,1024]{1,0:T(8,128)(2,1)} %get-tuple-element.133), kind=kOutput, calls=%fused_computation.8.clone.1 | convolution fusion | flops 1088421888 | bytes 9175072 | tf_op jit(solution)/shard_map/while/body/eval_jaxpr/phj,jhd->phd/dot_general | solution.py:45
  86.0 1.9 %collective-permute-done.1 = f32[128,1024]{0,1:T(8,128)S(1)} collective-permute-done((f32[128,1024]{0,1:T(8,128)}, f32[128,1024]{0,1:T(8,128)S(1)}, u32[]{:S(2)}, u32[]{:S(2)}) %collective-permute-start.1) | collective-permute-done | bytes 524320 | tf_op jit(solution)/shard_map/while/body/eval_jaxpr/ppermute | solution.py:20
  87.9 0.9 bitcast_add_fusion.2
  88.8 2.2 %fusion.37 = f32[128,512]{1,0:T(8,128)S(1)} fusion(f32[128,1024]{0,1:T(8,128)} %get-tuple-element.39, bf16[1024,512]{1,0:T(8,128)(2,1)} %param.22), kind=kOutput, calls=%fused_computation.50 | convolution fusion | flops 805306368 | bytes 1835008 | tf_op jit(solution)/shard_map/dot_general | solution.py:91
  91.0 9.6 %all_to_all.10 = f32[4,32,512]{2,1,0:T(8,128)S(1)} all-to-all(f32[4,32,512]{2,1,0:T(8,128)S(1)} %bitcast.126), channel_id=1, replica_groups=mesh['groups'=2,'obs'=4,'hid'=2,'rep'=2] {'obs'}, dimensions={0} | all-to-all | bytes 524288 | tf_op jit(solution)/shard_map/all_to_all | solution.py:95
  100.7 3.4 %all-to-all-start = ((f32[4,32,512]{2,1,0:T(8,128)}), f32[4,32,512]{2,1,0:T(8,128)S(1)}, u32[]{:S(2)}, u32[]{:S(2)}) async-start(f32[4,32,512]{2,1,0:T(8,128)} %bitcast.127), calls=%async_computation | async-start | bytes 524288 | tf_op jit(solution)/shard_map/all_to_all | solution.py:74
  104.1 1.2 fusion.38
  105.4 5.4 %all-to-all-done = f32[4,32,512]{2,1,0:T(8,128)S(1)} async-done(((f32[4,32,512]{2,1,0:T(8,128)}), f32[4,32,512]{2,1,0:T(8,128)S(1)}, u32[]{:S(2)}, u32[]{:S(2)}) %all-to-all-start) | async-done | bytes 262176 | tf_op jit(solution)/shard_map/all_to_all | solution.py:74
  110.8 1.7 %fusion.24 = f32[1,128,512]{2,1,0:T(8,128)S(1)} fusion(f32[1,128,512]{2,1,0:T(8,128)S(1)} %copy.60, s32[]{:T(128)S(6)} %select_n.2, bf16[1024,512]{1,0:T(8,128)(2,1)S(1)} %copy-done.7, bf16[512,1024]{1,0:T(8,128)(2,1)} %param.23, f32[1024]{0:T(1024)S(1)} %bitcast.130, f32[128,512]{1,0:T(8,128)S(1)} %bitcast.129, f32[128,512]{1,0:T(8,128)S(1)} %bitcast.125), kind=kOutput, calls=%fused_computation.31 | convolution fusion | flops 134676480 | bytes 2429952 | tf_op jit(solution)/shard_map/dot_general | solution.py:105
  112.6 0.7 copy-done.4
  113.4 16.1 %all-gather.2.cloned.1.call-done = f32[4,128,512]{2,1,0:T(8,128)} async-done(((f32[1,128,512]{2,1,0:T(8,128)}), f32[4,128,512]{2,1,0:T(8,128)}) %all-gather.2.cloned.1.call-update) | async-done | bytes 1048592 | tf_op jit(solution)/shard_map/all_gather | solution.py:14
  129.4 1.3 reduce_sum.9
  130.8 0.8 multiply_add_fusion
  (36 shorter events, 1.3 us)
Async XLA Ops:
  7.2 1.2 copy-start
  8.4 4.4 %copy-start.5 = (bf16[256,1024]{1,0:T(8,128)(2,1)S(1)}, bf16[256,1024]{1,0:T(8,128)(2,1)}, u32[]{:S(2)}) copy-start(bf16[256,1024]{1,0:T(8,128)(2,1)} %param.19) | copy-start | bytes 1572868
  12.8 3.3 %copy-start.3 = (f32[1,128,512]{2,1,0:T(8,128)S(1)}, f32[1,128,512]{2,1,0:T(8,128)}, u32[]{:S(2)}) copy-start(f32[1,128,512]{2,1,0:T(8,128)} %param.14) | copy-start | bytes 786436
  16.1 6.5 %copy-start.8 = (bf16[256,8]{0,1:T(8,128)(2,1)S(1)}, bf16[256,8]{0,1:T(8,128)(2,1)}, u32[]{:S(2)}) copy-start(bf16[256,8]{0,1:T(8,128)(2,1)} %param.21) | copy-start | bytes 12292
  16.1 6.6 %copy-start.1 = (bf16[512,1024]{1,0:T(8,128)(2,1)S(1)}, bf16[512,1024]{1,0:T(8,128)(2,1)}, u32[]{:S(2)}) copy-start(bf16[512,1024]{1,0:T(8,128)(2,1)} %param.18) | copy-start | bytes 3145732
  31.9 9.4 %collective-permute-start = (bf16[128,512]{1,0:T(8,128)(2,1)S(1)}, bf16[128,512]{1,0:T(8,128)(2,1)S(1)}, u32[]{:S(2)}, u32[]{:S(2)}) collective-permute-start(bf16[128,512]{1,0:T(8,128)(2,1)S(1)} %get-tuple-element.122), channel_id=1, source_target_pairs={{0,4},{4,8},{8,12},{12,0},{1,5},{5,9},{9,13},{13,1},{2,6},{6,10},{... | collective-permute-start | bytes 393224 | tf_op jit(solution)/shard_map/while/body/eval_jaxpr/ppermute | solution.py:20
  34.9 16.8 %collective-permute-start.1 = (f32[128,1024]{0,1:T(8,128)}, f32[128,1024]{0,1:T(8,128)S(1)}, u32[]{:S(2)}, u32[]{:S(2)}) collective-permute-start(f32[128,1024]{0,1:T(8,128)} %get-tuple-element.123), channel_id=1, source_target_pairs={{0,4},{4,8},{8,12},{12,0},{1,5},{5,9},{9,13},{13,1},{2,6},{6,10},{... | collective-permute-start | bytes 1572872 | tf_op jit(solution)/shard_map/while/body/eval_jaxpr/ppermute | solution.py:20
  52.5 8.2 %collective-permute-start = (bf16[128,512]{1,0:T(8,128)(2,1)S(1)}, bf16[128,512]{1,0:T(8,128)(2,1)S(1)}, u32[]{:S(2)}, u32[]{:S(2)}) collective-permute-start(bf16[128,512]{1,0:T(8,128)(2,1)S(1)} %get-tuple-element.122), channel_id=1, source_target_pairs={{0,4},{4,8},{8,12},{12,0},{1,5},{5,9},{9,13},{13,1},{2,6},{6,10},{... | collective-permute-start | bytes 393224 | tf_op jit(solution)/shard_map/while/body/eval_jaxpr/ppermute | solution.py:20
  52.6 17.7 %collective-permute-start.1 = (f32[128,1024]{0,1:T(8,128)}, f32[128,1024]{0,1:T(8,128)S(1)}, u32[]{:S(2)}, u32[]{:S(2)}) collective-permute-start(f32[128,1024]{0,1:T(8,128)} %get-tuple-element.123), channel_id=1, source_target_pairs={{0,4},{4,8},{8,12},{12,0},{1,5},{5,9},{9,13},{13,1},{2,6},{6,10},{... | collective-permute-start | bytes 1572872 | tf_op jit(solution)/shard_map/while/body/eval_jaxpr/ppermute | solution.py:20
  71.1 8.2 %collective-permute-start = (bf16[128,512]{1,0:T(8,128)(2,1)S(1)}, bf16[128,512]{1,0:T(8,128)(2,1)S(1)}, u32[]{:S(2)}, u32[]{:S(2)}) collective-permute-start(bf16[128,512]{1,0:T(8,128)(2,1)S(1)} %get-tuple-element.122), channel_id=1, source_target_pairs={{0,4},{4,8},{8,12},{12,0},{1,5},{5,9},{9,13},{13,1},{2,6},{6,10},{... | collective-permute-start | bytes 393224 | tf_op jit(solution)/shard_map/while/body/eval_jaxpr/ppermute | solution.py:20
  71.2 16.8 %collective-permute-start.1 = (f32[128,1024]{0,1:T(8,128)}, f32[128,1024]{0,1:T(8,128)S(1)}, u32[]{:S(2)}, u32[]{:S(2)}) collective-permute-start(f32[128,1024]{0,1:T(8,128)} %get-tuple-element.123), channel_id=1, source_target_pairs={{0,4},{4,8},{8,12},{12,0},{1,5},{5,9},{9,13},{13,1},{2,6},{6,10},{... | collective-permute-start | bytes 1572872 | tf_op jit(solution)/shard_map/while/body/eval_jaxpr/ppermute | solution.py:20
  88.8 22.0 %copy-start.7 = (bf16[1024,512]{1,0:T(8,128)(2,1)S(1)}, bf16[1024,512]{1,0:T(8,128)(2,1)}, u32[]{:S(2)}) copy-start(bf16[1024,512]{1,0:T(8,128)(2,1)} %param.25) | copy-start | bytes 3145732
  91.0 39.8 %copy-start.6 = (f32[4,32,512]{2,1,0:T(8,128)S(1)}, f32[4,32,512]{2,1,0:T(8,128)}, u32[]{:S(2)}) copy-start(f32[4,32,512]{2,1,0:T(8,128)} %param.17) | copy-start | bytes 786436
  100.7 10.2 %all-to-all-start = ((f32[4,32,512]{2,1,0:T(8,128)}), f32[4,32,512]{2,1,0:T(8,128)S(1)}, u32[]{:S(2)}, u32[]{:S(2)}) async-start(f32[4,32,512]{2,1,0:T(8,128)} %bitcast.127), calls=%async_computation | async-start | bytes 524288 | tf_op jit(solution)/shard_map/all_to_all | solution.py:74
  104.1 25.4 %all-gather.2.cloned.1.call-start = ((), (), s32[]{:S(2)}) async-start(), calls=%async_computation.2 | async-start | bytes 1310720 | tf_op jit(solution)/shard_map/all_gather | solution.py:14
  112.5 0.7 copy-start.4
  130.8 0.8 copy-start.2
Sparse Core Ops, SparseCore 0:
  113.4 15.9 all-gather.1
